TPU v7x, 32 devices: a whole 2x2x4 slice. The times are simulated.
32 devices in a mesh: chaos: 4 (over z), gx: 4 (over y, x), gy: 2 (over core).
Axes of the slice: x: 2, y: 2, z: 4, core: 2. Of those that a mesh axis runs over, the one named last changes fastest.
Arguments:
- lam_start: float32 [286, 16, 512], P(None, ('chaos', 'gy'), 'gx'), may hold values from -6 to 6
- adj_source: float32 [286, 16, 512], P(None, ('chaos', 'gy'), 'gx'), may hold values from -6 to 6
- coef_points: float32 [512, 4, 4, 512], P('chaos', None, 'gy', 'gx'), may hold values from 0.1 to 1
- quad_index: int32 [512, 10], replicated, may hold values from 0 to 3
- mode_index: int32 [286, 10], replicated, may hold values from 0 to 3, as said below
Outputs:
- lam_end: float32 [286, 16, 512], P(None, ('chaos', 'gy'), 'gx')
Inputs may be any that keep to these rules, and one draw needn't show every extreme that they name: `mode_index`: each row is a multi-index whose degrees sum to at most 3; each such multi-index of 10 inputs appears exactly once.
All inputs are finite; a program needn't handle non-finite values.
Results may differ from a plain program's by a relative error of at most 0.00011.
Values sent between devices are 32-bit elements; how exact they have to be, the bound alone decides.
A program may use at most 64 MiB of HBM per device.

v0:
```python
import math
import jax
import jax.numpy as jnp
from jax import lax
from jax.sharding import PartitionSpec as P

STEPS = 2
gauss_nodes = (-2.3344142183389773, -0.7419637843027259, 0.7419637843027259, 2.3344142183389773)
gauss_weights = (0.04587585476806849, 0.4541241452319315, 0.4541241452319315, 0.04587585476806849)
mass_shift = 1.0
relax_rate = 0.2
top_prec = lax.Precision.HIGHEST


def tables(quad_index, mode_index):
    node_vals = jnp.array(gauss_nodes, jnp.float32)
    node_wts = jnp.array(gauss_weights, jnp.float32)
    hermite = jnp.stack(
        [
            jnp.ones_like(node_vals),
            node_vals,
            (node_vals * node_vals - 1.0) / math.sqrt(2.0),
            (node_vals * node_vals * node_vals - 3.0 * node_vals) / math.sqrt(6.0),
        ],
        0,
    )
    levels = jnp.arange(4, dtype=jnp.int32)
    quad_hot = (quad_index[:, :, None] == levels[None, None, :]).astype(jnp.float32)
    mode_hot = (mode_index[:, :, None] == levels[None, None, :]).astype(jnp.float32)
    at_nodes = jnp.einsum("qdk,nk->qdn", quad_hot, hermite, precision=top_prec)
    factors = jnp.einsum("qdn,pdn->qpd", at_nodes, mode_hot, precision=top_prec)
    chaos_basis = jnp.prod(factors, axis=2)
    point_wts = jnp.prod(jnp.sum(quad_hot * node_wts[None, None, :], axis=2), axis=1)
    point_wts = point_wts / jnp.sum(point_wts)
    back_map = chaos_basis * point_wts[:, None]
    return (chaos_basis, back_map)


def shift_pair(low, high, axis):
    size = lax.axis_size(axis)
    up = [(i, (i + 1) % size) for i in range(size)]
    down = [(j, i) for i, j in up]
    return (lax.ppermute(high, axis, up), lax.ppermute(low, axis, down))


def local(lam_start, adj_source, coef_points, quad_index, mode_index):
    modes, row_len, col_len = lam_start.shape
    points = quad_index.shape[0]
    rows = ("chaos", "gy")
    row_dev = lax.axis_index(rows)
    row_devs = lax.axis_size(rows)
    keep_low = jnp.where(row_dev == 0, 0.0, 1.0).astype(jnp.float32)
    keep_high = jnp.where(row_dev == row_devs - 1, 0.0, 1.0).astype(jnp.float32)
    coef = lax.all_to_all(coef_points, "chaos", split_axis=1, concat_axis=0, tiled=True)
    coef = coef.reshape(points, row_len, col_len)
    k_low, k_high = shift_pair(coef[:, 0], coef[:, -1], rows)
    k_left, k_right = shift_pair(coef[:, :, :1], coef[:, :, -1:], "gx")
    chaos_basis, back_map = tables(quad_index, mode_index)
    coef_y = [k_low * keep_low] + [coef[:, r] for r in range(row_len)] + [k_high * keep_high]
    coef_x = [jnp.concatenate([k_left[:, r], coef[:, r], k_right[:, r]], 1) for r in range(row_len)]
    lam_now = lam_start
    for repeat in range(STEPS):
        v_low, v_high = shift_pair(lam_now[:, :2], lam_now[:, -2:], rows)
        v_left, v_right = shift_pair(lam_now[:, :, :2], lam_now[:, :, -2:], "gx")
        v_low = v_low * keep_low
        v_high = v_high * keep_high
        parts = (
            [v_low[:, 0], v_low[:, 1]]
            + [lam_now[:, r] for r in range(row_len)]
            + [v_high[:, 0], v_high[:, 1]]
        )
        edges = [v_left[:, r] for r in range(row_len)] + [v_right[:, r] for r in range(row_len)]
        u = jnp.dot(
            chaos_basis,
            jnp.concatenate(parts + edges, 1),
            precision=top_prec,
            preferred_element_type=jnp.float32,
        )
        u_row = [u[:, i * col_len : (i + 1) * col_len] for i in range(row_len + 4)]
        base = (row_len + 4) * col_len
        u_left = [u[:, base + 2 * r : base + 2 * r + 2] for r in range(row_len)]
        base += 2 * row_len
        u_right = [u[:, base + 2 * r : base + 2 * r + 2] for r in range(row_len)]
        flux_y = [coef_y[i] * ((u_row[i + 2] - u_row[i]) * 0.5) for i in range(row_len + 2)]
        div = []
        for r in range(row_len):
            wide = jnp.concatenate([u_left[r], u_row[r + 2], u_right[r]], 1)
            flux_x = coef_x[r] * ((wide[:, 2:] - wide[:, :-2]) * 0.5)
            div.append((flux_x[:, 2:] - flux_x[:, :-2]) * 0.5 + (flux_y[r + 2] - flux_y[r]) * 0.5)
        back = jnp.dot(
            back_map.T,
            jnp.concatenate(div, 1),
            precision=top_prec,
            preferred_element_type=jnp.float32,
        )
        divergence = back.reshape(modes, row_len, col_len)
        lam_now = lam_now + relax_rate * (adj_source - (mass_shift * lam_now - divergence))
    return lam_now


def solution(mesh):
    placed = (
        P(None, ("chaos", "gy"), "gx"),
        P(None, ("chaos", "gy"), "gx"),
        P("chaos", None, "gy", "gx"),
        P(),
        P(),
    )
    return jax.shard_map(
        local, mesh=mesh, in_specs=placed, out_specs=P(None, ("chaos", "gy"), "gx"), check_vma=False
    )
```

profile of v0, /device:TPU:0, one launch (start us, length us, event | category | flops | bytes accessed | tf_op | source)
XLA Modules:
  0.0 80.5 jit_solution(6977557665041020564)
XLA Ops:
  0.0 1.0 %copy.78 = f32[286,2,128]{2,0,1:T(8,128)S(1)} copy(f32[286,2,128]{2,1,0:T(2,128)} %param.7) | data formatting | bytes 585728 | tf_op args[0]
  1.0 4.5 %collective-permute-start.3 = (f32[286,2,128]{2,0,1:T(8,128)S(1)}, f32[286,2,128]{2,0,1:T(8,128)S(1)}, u32[]{:S(2)}, u32[]{:S(2)}) collective-permute-start(f32[286,2,128]{2,0,1:T(8,128)S(1)} %copy.78), channel_id=1, source_target_pairs={{1,0},{8,1},{9,8},{16,9},{17,16},{24,17},{25,24},{0,25},{3,2},{10,... | collective-permute-start | bytes 878600 | tf_op jit(solution)/shard_map/ppermute | solution.py:43
  5.5 2.0 %copy.67 = f32[128,4,2,128]{3,2,0,1:T(2,128)} copy(f32[128,4,2,128]{3,2,1,0:T(2,128)} %param.9) | data formatting | bytes 1048576 | tf_op args[2]
  7.6 3.6 %all-to-all-start = ((f32[128,4,2,128]{3,2,0,1:T(2,128)}), f32[128,4,2,128]{3,2,0,1:T(2,128)S(1)}, u32[]{:S(2)}, u32[]{:S(2)}) async-start(f32[128,4,2,128]{3,2,0,1:T(2,128)} %copy.67), calls=%async_computation | async-start | bytes 1048576 | tf_op jit(solution)/shard_map/all_to_all | solution.py:54
  11.2 0.1 fusion.64
  11.3 2.5 %collective-permute-start.5 = (f32[286,2,2]{2,0,1:T(8,128)S(1)}, f32[286,2,2]{2,0,1:T(8,128)S(1)}, u32[]{:S(2)}, u32[]{:S(2)}) collective-permute-start(f32[286,2,2]{2,0,1:T(8,128)S(1)} %get-tuple-element.35), channel_id=1, source_target_pairs={{2,0},{4,2},{6,4},{0,6},{3,1},{5,3},{7,5},{1,7},{10,8},{12,10},{14... | collective-permute-start | bytes 13736 | tf_op jit(solution)/shard_map/ppermute | solution.py:43
  13.9 0.1 select_reduce_fusion
  14.0 0.6 reduce_sum.19
  14.6 1.2 %broadcast_divide_fusion = f32[512]{0:T(512)} fusion(f32[512]{0:T(512)S(1)} %reduce_prod.19, f32[]{:T(128)} %reduce_sum.19), kind=kLoop, calls=%fused_computation.109 | loop fusion | flops 512 | bytes 4100 | tf_op jit(solution)/shard_map/div | solution.py:34
  15.9 0.2 fusion.54
  16.1 3.4 %convolution_reduce_fusion = f32[286,512]{1,0:T(8,128)S(1)} fusion(f32[512,10,4]{0,2,1:T(4,128)S(1)} %fusion.54, s32[286,10]{0,1:T(8,128)} %param.11), kind=kOutput, calls=%fused_computation | convolution fusion | flops 71616688 | bytes 679088 | tf_op jit(solution)/shard_map/qdn,pdn->qpd/dot_general | solution.py:31
  19.5 1.4 %collective-permute-done.5 = f32[286,2,2]{2,0,1:T(8,128)S(1)} collective-permute-done((f32[286,2,2]{2,0,1:T(8,128)S(1)}, f32[286,2,2]{2,0,1:T(8,128)S(1)}, u32[]{:S(2)}, u32[]{:S(2)}) %collective-permute-start.5) | collective-permute-done | bytes 4608 | tf_op jit(solution)/shard_map/ppermute | solution.py:43
  20.9 7.3 %collective-permute-done.4 = f32[286,2,2]{2,0,1:T(8,128)S(1)} collective-permute-done((f32[286,2,2]{2,0,1:T(8,128)S(1)}, f32[286,2,2]{2,0,1:T(8,128)S(1)}, u32[]{:S(2)}, u32[]{:S(2)}) %collective-permute-start.4) | collective-permute-done | bytes 4608 | tf_op jit(solution)/shard_map/ppermute | solution.py:43
  28.3 1.2 %concatenate.47 = f32[286,776]{1,0:T(8,128)} concatenate(f32[286,128]{1,0:T(8,128)S(1)} %get-tuple-element.44, f32[286,128]{1,0:T(8,128)S(1)} %get-tuple-element.43, f32[286,128]{1,0:T(8,128)S(1)} %get-tuple-element.42, f32[286,128]{1,0:T(8,128)S(1)} %get-tuple-element.41, f32[286,128]{1,0:T(8,128)S(1)} %get-tuple-element.40, f32[286,128]{1,0:T(8,128)S(1)} %get-tuple-element.39, ...), dimensions={1} | concatenate | bytes 1775488 | tf_op jit(solution)/shard_map/concatenate | solution.py:75
  29.5 3.9 %fusion.65 = f32[512,776]{0,1:T(8,128)S(1)} fusion(f32[286,512]{1,0:T(8,128)S(1)} %convolution_reduce_fusion, f32[286,776]{1,0:T(8,128)} %concatenate.47), kind=kOutput, calls=%fused_computation.118 | convolution fusion | flops 1363574784 | bytes 3062720 | tf_op jit(solution)/shard_map/dot_general | solution.py:73
  33.5 1.4 %fusion.62 = (f32[512,2,1]{2,1,0:T(2,128)S(1)}, f32[512,2,1]{2,1,0:T(2,128)}) fusion(f32[512,2,128]{2,1,0:T(2,128)S(1)} %bitcast.66), kind=kLoop, calls=%fused_computation.115 | loop fusion | bytes 16384 | tf_op jit(solution)/shard_map/slice | solution.py:57
  34.9 1.2 %copy.97 = f32[512,2,1]{0,2,1:T(1,128)S(1)} copy(f32[512,2,1]{2,1,0:T(2,128)} %get-tuple-element.20) | data formatting | bytes 8192
  36.1 1.5 %collective-permute-start.1 = (f32[512,2,1]{0,2,1:T(1,128)S(1)}, f32[512,2,1]{0,2,1:T(1,128)S(1)}, u32[]{:S(2)}, u32[]{:S(2)}) collective-permute-start(f32[512,2,1]{0,2,1:T(1,128)S(1)} %copy.97), channel_id=1, source_target_pairs={{2,0},{4,2},{6,4},{0,6},{3,1},{5,3},{7,5},{1,7},{10,8},{12,10},{14... | collective-permute-start | bytes 12296 | tf_op jit(solution)/shard_map/ppermute | solution.py:43
  37.6 1.2 %fusion.61 = (f32[512,1,128]{2,1,0:T(1,128)}, f32[512,1,128]{2,1,0:T(1,128)}) fusion(f32[512,2,128]{2,1,0:T(2,128)S(1)} %bitcast.67), kind=kLoop, calls=%fused_computation.114 | loop fusion | bytes 1048576 | tf_op jit(solution)/shard_map/slice | solution.py:60
  38.7 1.1 %copy.96 = f32[512,1,128]{0,2,1:T(8,128)S(1)} copy(f32[512,1,128]{2,1,0:T(1,128)} %get-tuple-element.17) | data formatting | bytes 524288
  39.8 1.1 %copy.98 = f32[512,1,128]{0,2,1:T(8,128)S(1)} copy(f32[512,1,128]{2,1,0:T(1,128)} %get-tuple-element.18) | data formatting | bytes 524288
  41.0 3.5 %collective-permute-start.7 = (f32[512,128]{0,1:T(8,128)S(1)}, f32[512,128]{0,1:T(8,128)}, u32[]{:S(2)}, u32[]{:S(2)}) collective-permute-start(f32[512,128]{0,1:T(8,128)S(1)} %bitcast.68), channel_id=1, source_target_pairs={{1,0},{8,1},{9,8},{16,9},{17,16},{24,17},{25,24},{0,25},{3,2},{10,... | collective-permute-start | bytes 786440 | tf_op jit(solution)/shard_map/ppermute | solution.py:43
  44.5 0.2 copy.95
  44.7 0.6 collective-permute-start
  45.3 3.9 %collective-permute-done = f32[512,2,1]{0,2,1:T(1,128)S(1)} collective-permute-done((f32[512,2,1]{0,2,1:T(1,128)S(1)}, f32[512,2,1]{0,2,1:T(1,128)S(1)}, u32[]{:S(2)}, u32[]{:S(2)}) %collective-permute-start) | collective-permute-done | bytes 4128 | tf_op jit(solution)/shard_map/ppermute | solution.py:43
  49.2 0.1 fusion.19
  49.3 0.5 copy-done.13
  49.8 1.1 %fusion.51 = (f32[512,128]{0,1:T(8,128)S(1)}, f32[512,128]{0,1:T(8,128)S(1)}) fusion(f32[512,776]{0,1:T(8,128)S(1)} %copy-done.1, f32[512,130]{0,1:T(8,128)S(1)} %fusion.19, f32[512,128]{0,1:T(8,128)} %collective-permute-done.6, f32[]{:T(128)S(6)} %select_n.7, f32[512,1,128]{0,2,1:T(8,128)S(1)} %copy.98), kind=kLoop, calls=%fused_computation.70 | loop fusion | flops 720896 | bytes 2621444 | tf_op jit(solution)/shard_map/add | solution.py:89
  51.1 1.2 %fusion.44 = f32[512,128]{0,1:T(8,128)S(1)} fusion(f32[512,776]{0,1:T(8,128)S(1)} %copy-done.1, f32[512,130]{0,1:T(8,128)S(1)} %fusion.21, f32[512,128]{0,1:T(8,128)} %collective-permute-done.7, f32[]{:T(128)S(6)} %select_n.8, f32[512,1,128]{0,2,1:T(8,128)S(1)} %copy.96), kind=kLoop, calls=%fused_computation.60 | loop fusion | flops 720896 | bytes 2097156 | tf_op jit(solution)/shard_map/add | solution.py:89
  52.3 0.7 fusion.2
  53.0 0.2 reshape.17
  53.3 0.1 fusion.63
  53.4 0.1 collective-permute-start.11
  53.5 2.1 %collective-permute-start.9 = (f32[286,2,128]{2,0,1:T(8,128)S(1)}, f32[286,2,128]{2,0,1:T(8,128)S(1)}, u32[]{:S(2)}, u32[]{:S(2)}) collective-permute-start(f32[286,2,128]{2,0,1:T(8,128)S(1)} %fusion.15), channel_id=1, source_target_pairs={{1,0},{8,1},{9,8},{16,9},{17,16},{24,17},{25,24},{0,25},{3,2},{10,... | collective-permute-start | bytes 878600 | tf_op jit(solution)/shard_map/ppermute | solution.py:43
  55.7 1.5 %collective-permute-start.10 = (f32[286,2,2]{2,0,1:T(8,128)S(1)}, f32[286,2,2]{2,0,1:T(8,128)S(1)}, u32[]{:S(2)}, u32[]{:S(2)}) collective-permute-start(f32[286,2,2]{2,0,1:T(8,128)S(1)} %get-tuple-element.24), channel_id=1, source_target_pairs={{0,2},{2,4},{4,6},{6,0},{1,3},{3,5},{5,7},{7,1},{8,10},{10,12},{12... | collective-permute-start | bytes 13736 | tf_op jit(solution)/shard_map/ppermute | solution.py:43
  57.2 6.2 %collective-permute-done.11 = f32[286,2,2]{2,0,1:T(8,128)S(1)} collective-permute-done((f32[286,2,2]{2,0,1:T(8,128)S(1)}, f32[286,2,2]{2,0,1:T(8,128)S(1)}, u32[]{:S(2)}, u32[]{:S(2)}) %collective-permute-start.11) | collective-permute-done | bytes 4608 | tf_op jit(solution)/shard_map/ppermute | solution.py:43
  63.3 6.4 %collective-permute-done.10 = f32[286,2,2]{2,0,1:T(8,128)S(1)} collective-permute-done((f32[286,2,2]{2,0,1:T(8,128)S(1)}, f32[286,2,2]{2,0,1:T(8,128)S(1)}, u32[]{:S(2)}, u32[]{:S(2)}) %collective-permute-start.10) | collective-permute-done | bytes 4608 | tf_op jit(solution)/shard_map/ppermute | solution.py:43
  69.8 0.7 slice_bitcast_fusion.2
  70.5 0.7 slice_bitcast_fusion.4
  71.2 0.7 slice_bitcast_fusion.8
  71.9 1.4 %concatenate.54 = f32[286,776]{1,0:T(8,128)S(1)} concatenate(f32[286,128]{1,0:T(8,128)} %get-tuple-element.32, f32[286,128]{1,0:T(8,128)} %get-tuple-element.31, f32[286,128]{1,0:T(8,128)S(1)} %get-tuple-element.30, f32[286,128]{1,0:T(8,128)S(1)} %get-tuple-element.29, f32[286,128]{1,0:T(8,128)} %get-tuple-element.28, f32[286,128]{1,0:T(8,128)} %get-tuple-element.27, ...), dimensions={1} | concatenate | bytes 1775488 | tf_op jit(solution)/shard_map/concatenate | solution.py:75
  73.3 2.7 %fusion.66 = f32[512,776]{0,1:T(8,128)S(1)} fusion(f32[286,512]{1,0:T(8,128)S(1)} %convolution_reduce_fusion, f32[286,776]{1,0:T(8,128)S(1)} %concatenate.54), kind=kOutput, calls=%fused_computation.119 | convolution fusion | flops 1363574784 | bytes 3062720 | tf_op jit(solution)/shard_map/dot_general | solution.py:73
  76.1 0.1 fusion.23
  76.2 1.1 %fusion.37 = (f32[512,128]{0,1:T(8,128)S(1)}, f32[512,128]{0,1:T(8,128)S(1)}) fusion(f32[512,776]{0,1:T(8,128)S(1)} %fusion.66, f32[512,130]{0,1:T(8,128)S(1)} %fusion.23, f32[512,128]{0,1:T(8,128)} %collective-permute-done.6, f32[]{:T(128)S(6)} %select_n.7, f32[512,1,128]{0,2,1:T(8,128)S(1)} %copy.98), kind=kLoop, calls=%fused_computation.50 | loop fusion | flops 720896 | bytes 2621444 | tf_op jit(solution)/shard_map/add | solution.py:89
  77.5 1.1 %fusion.30 = f32[512,128]{0,1:T(8,128)S(1)} fusion(f32[512,776]{0,1:T(8,128)S(1)} %fusion.66, f32[512,130]{0,1:T(8,128)S(1)} %fusion.25, f32[512,128]{0,1:T(8,128)} %collective-permute-done.7, f32[]{:T(128)S(6)} %select_n.8, f32[512,1,128]{0,2,1:T(8,128)S(1)} %copy.96), kind=kLoop, calls=%fused_computation.40 | loop fusion | flops 720896 | bytes 2097156 | tf_op jit(solution)/shard_map/add | solution.py:89
  78.6 0.7 fusion
  79.3 0.2 reshape.18
  79.5 0.9 %copy.89 = f32[286,2,128]{2,1,0:T(2,128)} copy(f32[286,2,128]{2,0,1:T(8,128)S(1)} %fusion.12) | data formatting | bytes 585728 | tf_op jit(solution)/shard_map/add | solution.py:97
  (68 shorter events, 0.7 us)
Async XLA Ops:
  1.0 27.2 %collective-permute-start.3 = (f32[286,2,128]{2,0,1:T(8,128)S(1)}, f32[286,2,128]{2,0,1:T(8,128)S(1)}, u32[]{:S(2)}, u32[]{:S(2)}) collective-permute-start(f32[286,2,128]{2,0,1:T(8,128)S(1)} %copy.78), channel_id=1, source_target_pairs={{1,0},{8,1},{9,8},{16,9},{17,16},{24,17},{25,24},{0,25},{3,2},{10,... | collective-permute-start | bytes 878600 | tf_op jit(solution)/shard_map/ppermute | solution.py:43
  5.5 22.7 %collective-permute-start.2 = (f32[286,2,128]{2,0,1:T(8,128)S(1)}, f32[286,2,128]{2,0,1:T(8,128)S(1)}, u32[]{:S(2)}, u32[]{:S(2)}) collective-permute-start(f32[286,2,128]{2,0,1:T(8,128)S(1)} %copy.78), channel_id=1, source_target_pairs={{0,1},{1,8},{8,9},{9,16},{16,17},{17,24},{24,25},{25,0},{2,3},{3,1... | collective-permute-start | bytes 878600 | tf_op jit(solution)/shard_map/ppermute | solution.py:43
  7.6 6.3 %copy-start.4 = (s32[512,10]{0,1:T(8,128)S(1)}, s32[512,10]{0,1:T(8,128)}, u32[]{:S(2)}) copy-start(s32[512,10]{0,1:T(8,128)} %param.10) | copy-start | bytes 61444
  7.6 6.3 %copy-start.16 = (f32[4]{0:T(128)S(1)}, f32[4]{0:T(128)}, u32[]{:S(2)}) copy-start(f32[4]{0:T(128)} %constant.42.clone) | copy-start | bytes 52
  7.6 8.3 %copy-start.15 = (f32[4,4,1]{1,0,2:T(4,128)S(1)}, f32[4,4,1]{1,0,2:T(4,128)}, u32[]{:S(2)}) copy-start(f32[4,4,1]{1,0,2:T(4,128)} %constant.56) | copy-start | bytes 196
  7.6 25.9 %all-to-all-start = ((f32[128,4,2,128]{3,2,0,1:T(2,128)}), f32[128,4,2,128]{3,2,0,1:T(2,128)S(1)}, u32[]{:S(2)}, u32[]{:S(2)}) async-start(f32[128,4,2,128]{3,2,0,1:T(2,128)} %copy.67), calls=%async_computation | async-start | bytes 1048576 | tf_op jit(solution)/shard_map/all_to_all | solution.py:54
  11.3 9.5 %collective-permute-start.5 = (f32[286,2,2]{2,0,1:T(8,128)S(1)}, f32[286,2,2]{2,0,1:T(8,128)S(1)}, u32[]{:S(2)}, u32[]{:S(2)}) collective-permute-start(f32[286,2,2]{2,0,1:T(8,128)S(1)} %get-tuple-element.35), channel_id=1, source_target_pairs={{2,0},{4,2},{6,4},{0,6},{3,1},{5,3},{7,5},{1,7},{10,8},{12,10},{14... | collective-permute-start | bytes 13736 | tf_op jit(solution)/shard_map/ppermute | solution.py:43
  13.8 14.3 %collective-permute-start.4 = (f32[286,2,2]{2,0,1:T(8,128)S(1)}, f32[286,2,2]{2,0,1:T(8,128)S(1)}, u32[]{:S(2)}, u32[]{:S(2)}) collective-permute-start(f32[286,2,2]{2,0,1:T(8,128)S(1)} %get-tuple-element.36), channel_id=1, source_target_pairs={{0,2},{2,4},{4,6},{6,0},{1,3},{3,5},{5,7},{7,1},{8,10},{10,12},{12... | collective-permute-start | bytes 13736 | tf_op jit(solution)/shard_map/ppermute | solution.py:43
  33.5 2.6 %copy-start = (f32[512,776]{0,1:T(8,128)}, f32[512,776]{0,1:T(8,128)S(1)}, u32[]{:S(2)}) copy-start(f32[512,776]{0,1:T(8,128)S(1)} %fusion.65) | copy-start | bytes 4767748
  36.1 9.2 %collective-permute-start.1 = (f32[512,2,1]{0,2,1:T(1,128)S(1)}, f32[512,2,1]{0,2,1:T(1,128)S(1)}, u32[]{:S(2)}, u32[]{:S(2)}) collective-permute-start(f32[512,2,1]{0,2,1:T(1,128)S(1)} %copy.97), channel_id=1, source_target_pairs={{2,0},{4,2},{6,4},{0,6},{3,1},{5,3},{7,5},{1,7},{10,8},{12,10},{14... | collective-permute-start | bytes 12296 | tf_op jit(solution)/shard_map/ppermute | solution.py:43
  37.6 11.7 %slice-start = ((f32[512,776]{0,1:T(8,128)}), f32[512,128]{0,1:T(8,128)S(1)}, s32[]{:S(2)}) async-start(f32[512,776]{0,1:T(8,128)} %copy-done), calls=%async_computation.1 | async-start | bytes 524288 | tf_op jit(solution)/shard_map/slice | solution.py:79
  37.6 12.3 %copy-start.1 = (f32[512,776]{0,1:T(8,128)S(1)}, f32[512,776]{0,1:T(8,128)}, u32[]{:S(2)}) copy-start(f32[512,776]{0,1:T(8,128)} %copy-done) | copy-start | bytes 4767748
  40.9 8.9 %collective-permute-start.6 = (f32[512,128]{0,1:T(8,128)S(1)}, f32[512,128]{0,1:T(8,128)}, u32[]{:S(2)}, u32[]{:S(2)}) collective-permute-start(f32[512,128]{0,1:T(8,128)S(1)} %bitcast.71), channel_id=1, source_target_pairs={{0,1},{1,8},{8,9},{9,16},{16,17},{17,24},{24,25},{25,0},{2,3},{3,1... | collective-permute-start | bytes 786440 | tf_op jit(solution)/shard_map/ppermute | solution.py:43
  41.0 10.1 %collective-permute-start.7 = (f32[512,128]{0,1:T(8,128)S(1)}, f32[512,128]{0,1:T(8,128)}, u32[]{:S(2)}, u32[]{:S(2)}) collective-permute-start(f32[512,128]{0,1:T(8,128)S(1)} %bitcast.68), channel_id=1, source_target_pairs={{1,0},{8,1},{9,8},{16,9},{17,16},{24,17},{25,24},{0,25},{3,2},{10,... | collective-permute-start | bytes 786440 | tf_op jit(solution)/shard_map/ppermute | solution.py:43
  44.7 4.5 %collective-permute-start = (f32[512,2,1]{0,2,1:T(1,128)S(1)}, f32[512,2,1]{0,2,1:T(1,128)S(1)}, u32[]{:S(2)}, u32[]{:S(2)}) collective-permute-start(f32[512,2,1]{0,2,1:T(1,128)S(1)} %copy.95), channel_id=1, source_target_pairs={{0,2},{2,4},{4,6},{6,0},{1,3},{3,5},{5,7},{7,1},{8,10},{10,12},{12... | collective-permute-start | bytes 12296 | tf_op jit(solution)/shard_map/ppermute | solution.py:43
  45.3 4.0 %copy-start.11 = (f32[512,1]{0,1:T(1,128)}, f32[512,1]{0,1:T(1,128)S(1)}, u32[]{:S(2)}) copy-start(f32[512,1]{0,1:T(1,128)S(1)} %get-tuple-element.47) | copy-start | bytes 6148
  45.3 5.7 %copy-start.7 = (f32[512,1]{0,1:T(1,128)}, f32[512,1]{0,1:T(1,128)S(1)}, u32[]{:S(2)}) copy-start(f32[512,1]{0,1:T(1,128)S(1)} %get-tuple-element.48) | copy-start | bytes 6148
  49.2 0.6 copy-start.13
  49.2 1.8 %copy-start.9 = (f32[512,1]{0,1:T(1,128)}, f32[512,1]{0,1:T(1,128)S(1)}, u32[]{:S(2)}) copy-start(f32[512,1]{0,1:T(1,128)S(1)} %get-tuple-element.46) | copy-start | bytes 6148
  51.0 1.3 %copy-start.5 = (f32[512]{0:T(512)S(1)}, f32[512]{0:T(512)}, u32[]{:S(2)}) copy-start(f32[512]{0:T(512)} %broadcast_divide_fusion) | copy-start | bytes 6148
  51.1 2.1 %copy-start.2 = (f32[286,2,128]{2,1,0:T(2,128)S(1)}, f32[286,2,128]{2,1,0:T(2,128)}, u32[]{:S(2)}) copy-start(f32[286,2,128]{2,1,0:T(2,128)} %param.7) | copy-start | bytes 878596
  51.1 2.1 %copy-start.3 = (f32[286,2,128]{2,1,0:T(2,128)S(1)}, f32[286,2,128]{2,1,0:T(2,128)}, u32[]{:S(2)}) copy-start(f32[286,2,128]{2,1,0:T(2,128)} %param.8) | copy-start | bytes 878596
  53.4 9.9 %collective-permute-start.11 = (f32[286,2,2]{2,0,1:T(8,128)S(1)}, f32[286,2,2]{2,0,1:T(8,128)S(1)}, u32[]{:S(2)}, u32[]{:S(2)}) collective-permute-start(f32[286,2,2]{2,0,1:T(8,128)S(1)} %get-tuple-element.23), channel_id=1, source_target_pairs={{2,0},{4,2},{6,4},{0,6},{3,1},{5,3},{7,5},{1,7},{10,8},{12,10},{14... | collective-permute-start | bytes 13736 | tf_op jit(solution)/shard_map/ppermute | solution.py:43
  53.5 16.9 %collective-permute-start.9 = (f32[286,2,128]{2,0,1:T(8,128)S(1)}, f32[286,2,128]{2,0,1:T(8,128)S(1)}, u32[]{:S(2)}, u32[]{:S(2)}) collective-permute-start(f32[286,2,128]{2,0,1:T(8,128)S(1)} %fusion.15), channel_id=1, source_target_pairs={{1,0},{8,1},{9,8},{16,9},{17,16},{24,17},{25,24},{0,25},{3,2},{10,... | collective-permute-start | bytes 878600 | tf_op jit(solution)/shard_map/ppermute | solution.py:43
  55.7 15.5 %collective-permute-start.8 = (f32[286,2,128]{2,0,1:T(8,128)S(1)}, f32[286,2,128]{2,0,1:T(8,128)S(1)}, u32[]{:S(2)}, u32[]{:S(2)}) collective-permute-start(f32[286,2,128]{2,0,1:T(8,128)S(1)} %fusion.15), channel_id=1, source_target_pairs={{0,1},{1,8},{8,9},{9,16},{16,17},{17,24},{24,25},{25,0},{2,3},{3,1... | collective-permute-start | bytes 878600 | tf_op jit(solution)/shard_map/ppermute | solution.py:43
  55.7 14.1 %collective-permute-start.10 = (f32[286,2,2]{2,0,1:T(8,128)S(1)}, f32[286,2,2]{2,0,1:T(8,128)S(1)}, u32[]{:S(2)}, u32[]{:S(2)}) collective-permute-start(f32[286,2,2]{2,0,1:T(8,128)S(1)} %get-tuple-element.24), channel_id=1, source_target_pairs={{0,2},{2,4},{4,6},{6,0},{1,3},{3,5},{5,7},{7,1},{8,10},{10,12},{12... | collective-permute-start | bytes 13736 | tf_op jit(solution)/shard_map/ppermute | solution.py:43
  73.3 2.8 %copy-start.12 = (f32[512,1]{0,1:T(1,128)S(1)}, f32[512,1]{0,1:T(1,128)}, u32[]{:S(2)}) copy-start(f32[512,1]{0,1:T(1,128)} %copy-done.11) | copy-start | bytes 6148
  73.3 2.8 %copy-start.14 = (f32[512,1]{0,1:T(1,128)S(1)}, f32[512,1]{0,1:T(1,128)}, u32[]{:S(2)}) copy-start(f32[512,1]{0,1:T(1,128)} %copy-done.13) | copy-start | bytes 6148
  76.1 1.3 %copy-start.8 = (f32[512,1]{0,1:T(1,128)S(1)}, f32[512,1]{0,1:T(1,128)}, u32[]{:S(2)}) copy-start(f32[512,1]{0,1:T(1,128)} %copy-done.7) | copy-start | bytes 6148
  76.1 1.3 %copy-start.10 = (f32[512,1]{0,1:T(1,128)S(1)}, f32[512,1]{0,1:T(1,128)}, u32[]{:S(2)}) copy-start(f32[512,1]{0,1:T(1,128)} %copy-done.9) | copy-start | bytes 6148
  77.4 1.2 %copy-start.6 = (f32[512]{0:T(512)S(1)}, f32[512]{0:T(512)}, u32[]{:S(2)}) copy-start(f32[512]{0:T(512)} %broadcast_divide_fusion) | copy-start | bytes 6148
where the time goes:
time: 81.1 us; the launch traced here: 80.5 us
  waiting for transfers between devices  25.1 us (31%)
  starting transfers between devices  20 us (25%)
  local copies, waits for them, and re-layouts  16.1 us (20%)
  matrix products  11.6 us (14%)
  other arithmetic  7.13 us (9%)
    ppermute x12, waiting for transfers between devices, shift_pair(): return (lax.ppermute(high, axis, up), lax.ppermute(low, axis, down))  25.1 us
    ppermute x12, starting transfers between devices, shift_pair(): return (lax.ppermute(high, axis, up), lax.ppermute(low, axis, down))  16.4 us
    unnamed x40, local copies, waits for them, and re-layouts  7.13 us
    dot_general x2, matrix products, local(): jnp.dot(chaos_basis, jnp.concatenate(parts + edges, 1), precision=top_pre...  6.67 us
    add x4, other arithmetic, local(): (flux_x[:, 2:] - flux_x[:, :-2]) * 0.5 + (flux_y[r + 2] - flux_y[r]) * 0.5  4.61 us
    all_to_all x1, starting transfers between devices, local(): lax.all_to_all(coef_points, 'chaos', split_axis=1, concat_axis=0, tiled=T...  3.6 us
    dot_general x1, matrix products, tables(): factors = jnp.einsum('qdn,pdn->qpd', at_nodes, mode_hot, precision=top_prec)  3.4 us
    concatenate x2, local copies, waits for them, and re-layouts, local(): jnp.concatenate(parts + edges, 1)  2.57 us
  transfers between devices with their start and end apart: 13, of which 5 were waited for; matrix products, arithmetic and copies ran while one was open for 24% of the time, Pallas kernels for 0%

commit v1 on v0

--- a/solution.py
+++ b/solution.py
@@ -10,6 +10,18 @@
 mass_shift = 1.0
 relax_rate = 0.2
 top_prec = lax.Precision.HIGHEST
+
+
+def cut_along(x, dim, length):
+    shape = x.shape
+    tiles = x.reshape(*shape[:dim], length, shape[dim] // length, *shape[dim + 1 :])
+    return jnp.moveaxis(tiles, dim, 0)
+
+
+def laid_out(tiles, dim):
+    tiles = jnp.moveaxis(tiles, 0, dim)
+    lengths = tiles.shape
+    return tiles.reshape(*lengths[:dim], lengths[dim] * lengths[dim + 1], *lengths[dim + 2 :])
 
 
 def tables(quad_index, mode_index):
@@ -51,7 +63,15 @@
     row_devs = lax.axis_size(rows)
     keep_low = jnp.where(row_dev == 0, 0.0, 1.0).astype(jnp.float32)
     keep_high = jnp.where(row_dev == row_devs - 1, 0.0, 1.0).astype(jnp.float32)
-    coef = lax.all_to_all(coef_points, "chaos", split_axis=1, concat_axis=0, tiled=True)
+    size_2, here = (lax.axis_size("chaos"), lax.axis_index("chaos"))
+    blocks = cut_along(coef_points, 1, size_2)
+    result = blocks
+    for step in range(1, size_2):
+        target, source = ((here + step) % size_2, (here - step) % size_2)
+        sent = lax.dynamic_index_in_dim(blocks, target, 0)
+        other = lax.ppermute(sent, "chaos", [(i_2, (i_2 + step) % size_2) for i_2 in range(size_2)])
+        result = lax.dynamic_update_slice_in_dim(result, other, source, axis=0)
+    coef = laid_out(result, 0)
     coef = coef.reshape(points, row_len, col_len)
     k_low, k_high = shift_pair(coef[:, 0], coef[:, -1], rows)
     k_left, k_right = shift_pair(coef[:, :, :1], coef[:, :, -1:], "gx")

time: 81.1 us -> 78.3 us (0.965)
  other arithmetic: 7.13 us -> 4.62 us
  waiting for transfers between devices: 25.1 us -> 27.4 us
  matrix products: 11.6 us -> 9.62 us
    ppermute x0 -> x3, waiting for transfers between devices: none -> 7.84 us  [local(): lax.ppermute(sent, 'chaos', [(i_2, (i_2 + step) % size_2) for i_2 in rang...]
    ppermute x12, waiting for transfers between devices: 25.1 us -> 19.6 us  [shift_pair(): return (lax.ppermute(high, axis, up), lax.ppermute(low, axis, down))]
    unnamed x40 -> x18, local copies, waits for them, and re-layouts: 7.13 us -> 3.28 us
    add x4 -> x2, other arithmetic: 4.61 us -> 0.77 us  [local(): (flux_x[:, 2:] - flux_x[:, :-2]) * 0.5 + (flux_y[r + 2] - flux_y[r]) * 0.5]
    all_to_all x1 -> x0, starting transfers between devices: 3.6 us -> none  [local(): lax.all_to_all(coef_points, 'chaos', split_axis=1, concat_axis=0, tiled=T...]
    ppermute x0 -> x3, starting transfers between devices: none -> 2.08 us  [local(): lax.ppermute(sent, 'chaos', [(i_2, (i_2 + step) % size_2) for i_2 in rang...]
    ppermute x12, starting transfers between devices: 16.4 us -> 18.3 us  [shift_pair(): return (lax.ppermute(high, axis, up), lax.ppermute(low, axis, down))]
    squeeze x2, local copies, waits for them, and re-layouts: 0.04 us -> 1.47 us  [local(): v_right[:, r]]
  transfers between devices with their start and end apart: 13 -> 15, of which waited for: 5 -> 7; matrix products, arithmetic and copies ran while one was open for 24% -> 22% of each run, Pallas kernels for 0% -> 0%
where the time goes in v1:
time: 78.3 us; the launch traced here: 77.9 us
  waiting for transfers between devices  27.4 us (35%)
  starting transfers between devices  20.4 us (26%)
  local copies, waits for them, and re-layouts  15.4 us (20%)
  matrix products  9.62 us (12%)
  other arithmetic  4.62 us (6%)
    ppermute x12, waiting for transfers between devices, shift_pair(): return (lax.ppermute(high, axis, up), lax.ppermute(low, axis, down))  19.6 us
    ppermute x12, starting transfers between devices, shift_pair(): return (lax.ppermute(high, axis, up), lax.ppermute(low, axis, down))  18.3 us
    ppermute x3, waiting for transfers between devices, local(): lax.ppermute(sent, 'chaos', [(i_2, (i_2 + step) % size_2) for i_2 in rang...  7.84 us
    dot_general x2, matrix products, local(): jnp.dot(chaos_basis, jnp.concatenate(parts + edges, 1), precision=top_pre...  5.45 us
    unnamed x18, local copies, waits for them, and re-layouts  3.28 us
    concatenate x2, local copies, waits for them, and re-layouts, local(): jnp.concatenate(parts + edges, 1)  3.07 us
    dot_general x1, matrix products, tables(): factors = jnp.einsum('qdn,pdn->qpd', at_nodes, mode_hot, precision=top_prec)  2.62 us
    ppermute x3, starting transfers between devices, local(): lax.ppermute(sent, 'chaos', [(i_2, (i_2 + step) % size_2) for i_2 in rang...  2.08 us
  transfers between devices with their start and end apart: 15, of which 7 were waited for; matrix products, arithmetic and copies ran while one was open for 22% of the time, Pallas kernels for 0%

profile of v1, /device:TPU:0, one launch (start us, length us, event | category | flops | bytes accessed | tf_op | source)
XLA Modules:
  0.0 77.9 jit_solution(11885158355449301248)
XLA Ops:
  0.0 1.0 %copy.91 = f32[128,4,2,128]{3,2,1,0:T(2,128)S(1)} copy(f32[128,4,2,128]{3,2,1,0:T(2,128)} %param.9) | data formatting | bytes 1048576
  1.0 1.0 %copy.54 = f32[286,2,128]{2,0,1:T(8,128)S(1)} copy(f32[286,2,128]{2,1,0:T(2,128)} %param.7) | data formatting | bytes 585728 | tf_op args[0]
  2.1 4.5 %collective-permute-start.6 = (f32[286,2,128]{2,0,1:T(8,128)S(1)}, f32[286,2,128]{2,0,1:T(8,128)}, u32[]{:S(2)}, u32[]{:S(2)}) collective-permute-start(f32[286,2,128]{2,0,1:T(8,128)S(1)} %copy.54), channel_id=1, source_target_pairs={{1,0},{8,1},{9,8},{16,9},{17,16},{24,17},{25,24},{0,25},{3,2},{10,... | collective-permute-start | bytes 878600 | tf_op jit(solution)/shard_map/ppermute | solution.py:55
  6.7 1.1 %collective-permute-start.2 = (f32[1,128,1,2,128]{4,3,0,1,2:T(2,128)S(1)}, f32[1,128,1,2,128]{4,3,0,1,2:T(2,128)S(1)}, u32[]{:S(2)}, u32[]{:S(2)}) collective-permute-start(f32[1,128,1,2,128]{4,3,0,1,2:T(2,128)S(1)} %get-tuple-element.25), channel_id=1, source_target_pairs={{0,24},{8,0},{16,8},{24,16},{1,25},{9,1},{17,9},{25,17},{2,26},{10... | collective-permute-start | bytes 393224 | tf_op jit(solution)/shard_map/ppermute | solution.py:72
  7.9 1.0 %collective-permute-start = (f32[1,128,1,2,128]{4,3,0,1,2:T(2,128)S(1)}, f32[1,128,1,2,128]{4,3,0,1,2:T(2,128)S(1)}, u32[]{:S(2)}, u32[]{:S(2)}) collective-permute-start(f32[1,128,1,2,128]{4,3,0,1,2:T(2,128)S(1)} %get-tuple-element.26), channel_id=1, source_target_pairs={{0,8},{8,16},{16,24},{24,0},{1,9},{9,17},{17,25},{25,1},{2,10},{10... | collective-permute-start | bytes 393224 | tf_op jit(solution)/shard_map/ppermute | solution.py:72
  9.0 2.5 %collective-permute-start.8 = (f32[286,2,2]{2,0,1:T(8,128)S(1)}, f32[286,2,2]{2,0,1:T(8,128)S(1)}, u32[]{:S(2)}, u32[]{:S(2)}) collective-permute-start(f32[286,2,2]{2,0,1:T(8,128)S(1)} %get-tuple-element.42), channel_id=1, source_target_pairs={{2,0},{4,2},{6,4},{0,6},{3,1},{5,3},{7,5},{1,7},{10,8},{12,10},{14... | collective-permute-start | bytes 13736 | tf_op jit(solution)/shard_map/ppermute | solution.py:55
  11.7 0.6 reduce_sum.19
  12.3 0.6 broadcast_divide_fusion
  12.9 0.2 fusion.54
  13.1 2.6 %convolution_reduce_fusion = f32[286,512]{1,0:T(8,128)S(1)} fusion(f32[512,10,4]{0,2,1:T(4,128)S(1)} %fusion.54, s32[286,10]{0,1:T(8,128)S(1)} %copy-done.7), kind=kOutput, calls=%fused_computation | convolution fusion | flops 71616688 | bytes 679088 | tf_op jit(solution)/shard_map/qdn,pdn->qpd/dot_general | solution.py:43
  15.9 2.4 %collective-permute-done.8 = f32[286,2,2]{2,0,1:T(8,128)S(1)} collective-permute-done((f32[286,2,2]{2,0,1:T(8,128)S(1)}, f32[286,2,2]{2,0,1:T(8,128)S(1)}, u32[]{:S(2)}, u32[]{:S(2)}) %collective-permute-start.8) | collective-permute-done | bytes 4608 | tf_op jit(solution)/shard_map/ppermute | solution.py:55
  18.3 2.4 %collective-permute-start.7 = (f32[286,2,2]{2,0,1:T(8,128)S(1)}, f32[286,2,2]{2,0,1:T(8,128)S(1)}, u32[]{:S(2)}, u32[]{:S(2)}) collective-permute-start(f32[286,2,2]{2,0,1:T(8,128)S(1)} %get-tuple-element.43), channel_id=1, source_target_pairs={{0,2},{2,4},{4,6},{6,0},{1,3},{3,5},{5,7},{7,1},{8,10},{10,12},{12... | collective-permute-start | bytes 13736 | tf_op jit(solution)/shard_map/ppermute | solution.py:55
  20.7 0.7 slice_bitcast_fusion.12
  21.4 7.8 %collective-permute-done.7 = f32[286,2,2]{2,0,1:T(8,128)S(1)} collective-permute-done((f32[286,2,2]{2,0,1:T(8,128)S(1)}, f32[286,2,2]{2,0,1:T(8,128)S(1)}, u32[]{:S(2)}, u32[]{:S(2)}) %collective-permute-start.7) | collective-permute-done | bytes 4608 | tf_op jit(solution)/shard_map/ppermute | solution.py:55
  29.2 0.7 slice_bitcast_fusion.14
  30.0 7.8 %collective-permute-done.1 = f32[1,128,1,2,128]{4,3,0,1,2:T(2,128)S(1)} collective-permute-done((f32[1,128,1,2,128]{4,3,0,1,2:T(2,128)S(1)}, f32[1,128,1,2,128]{4,3,0,1,2:T(2,128)S(1)}, u32[]{:S(2)}, u32[]{:S(2)}) %collective-permute-start.1) | collective-permute-done | bytes 131104 | tf_op jit(solution)/shard_map/ppermute | solution.py:72
  38.0 0.3 copy.44
  38.3 0.2 reshape_reshape.3
  38.5 1.0 %collective-permute-start.3 = (f32[512,2,1]{0,2,1:T(1,128)S(1)}, f32[512,2,1]{0,2,1:T(1,128)S(1)}, u32[]{:S(2)}, u32[]{:S(2)}) collective-permute-start(f32[512,2,1]{0,2,1:T(1,128)S(1)} %get-tuple-element.23), channel_id=1, source_target_pairs={{0,2},{2,4},{4,6},{6,0},{1,3},{3,5},{5,7},{7,1},{8,10},{10,12},{12... | collective-permute-start | bytes 12296 | tf_op jit(solution)/shard_map/ppermute | solution.py:55
  39.5 2.1 %collective-permute-start.4 = (f32[512,2,1]{0,2,1:T(1,128)S(1)}, f32[512,2,1]{0,2,1:T(1,128)S(1)}, u32[]{:S(2)}, u32[]{:S(2)}) collective-permute-start(f32[512,2,1]{0,2,1:T(1,128)S(1)} %get-tuple-element.24), channel_id=1, source_target_pairs={{2,0},{4,2},{6,4},{0,6},{3,1},{5,3},{7,5},{1,7},{10,8},{12,10},{14... | collective-permute-start | bytes 12296 | tf_op jit(solution)/shard_map/ppermute | solution.py:55
  41.6 0.6 collective-permute-start.10
  42.2 0.9 %collective-permute-done.3 = f32[512,2,1]{0,2,1:T(1,128)S(1)} collective-permute-done((f32[512,2,1]{0,2,1:T(1,128)S(1)}, f32[512,2,1]{0,2,1:T(1,128)S(1)}, u32[]{:S(2)}, u32[]{:S(2)}) %collective-permute-start.3) | collective-permute-done | bytes 4128 | tf_op jit(solution)/shard_map/ppermute | solution.py:55
  43.2 1.0 %broadcast_multiply_fusion.1 = f32[286,2,128]{2,0,1:T(8,128)S(1)} fusion(f32[286,2,128]{2,0,1:T(8,128)} %collective-permute-done.6, f32[]{:T(128)S(6)} %select_n.66), kind=kLoop, calls=%fused_computation.98 | loop fusion | flops 73216 | bytes 585732 | tf_op jit(solution)/shard_map/mul | solution.py:86
  44.2 0.7 slice_bitcast_fusion.16
  44.9 1.0 %broadcast_multiply_fusion.3 = f32[286,2,128]{2,0,1:T(8,128)S(1)} fusion(f32[286,2,128]{2,0,1:T(8,128)} %collective-permute-done.5, f32[]{:T(128)S(6)} %select_n.65), kind=kLoop, calls=%fused_computation.100 | loop fusion | flops 73216 | bytes 585732 | tf_op jit(solution)/shard_map/mul | solution.py:85
  45.9 0.7 slice_bitcast_fusion.20
  46.6 1.5 %concatenate.47 = f32[286,776]{1,0:T(8,128)S(1)} concatenate(f32[286,128]{1,0:T(8,128)} %get-tuple-element.51, f32[286,128]{1,0:T(8,128)} %get-tuple-element.50, f32[286,128]{1,0:T(8,128)S(1)} %get-tuple-element.49, f32[286,128]{1,0:T(8,128)S(1)} %get-tuple-element.48, f32[286,128]{1,0:T(8,128)} %get-tuple-element.47, f32[286,128]{1,0:T(8,128)} %get-tuple-element.46, ...), dimensions={1} | concatenate | bytes 1775488 | tf_op jit(solution)/shard_map/concatenate | solution.py:95
  48.1 2.7 %fusion.66 = f32[512,776]{0,1:T(8,128)S(1)} fusion(f32[286,512]{1,0:T(8,128)S(1)} %convolution_reduce_fusion, f32[286,776]{1,0:T(8,128)S(1)} %concatenate.47), kind=kOutput, calls=%fused_computation.127 | convolution fusion | flops 1363574784 | bytes 3062720 | tf_op jit(solution)/shard_map/dot_general | solution.py:93
  51.1 0.4 fusion.51
  51.5 0.3 copy-done.2
  51.8 0.7 fusion.2
  53.1 3.0 %collective-permute-start.14 = (f32[286,2,2]{2,0,1:T(8,128)S(1)}, f32[286,2,2]{2,0,1:T(8,128)S(1)}, u32[]{:S(2)}, u32[]{:S(2)}) collective-permute-start(f32[286,2,2]{2,0,1:T(8,128)S(1)} %get-tuple-element.30), channel_id=1, source_target_pairs={{2,0},{4,2},{6,4},{0,6},{3,1},{5,3},{7,5},{1,7},{10,8},{12,10},{14... | collective-permute-start | bytes 13736 | tf_op jit(solution)/shard_map/ppermute | solution.py:55
  56.0 0.7 slice_bitcast_fusion.8
  56.8 1.2 %collective-permute-start.12 = (f32[286,2,128]{2,0,1:T(8,128)S(1)}, f32[286,2,128]{2,0,1:T(8,128)S(1)}, u32[]{:S(2)}, u32[]{:S(2)}) collective-permute-start(f32[286,2,128]{2,0,1:T(8,128)S(1)} %fusion.15), channel_id=1, source_target_pairs={{1,0},{8,1},{9,8},{16,9},{17,16},{24,17},{25,24},{0,25},{3,2},{10,... | collective-permute-start | bytes 878600 | tf_op jit(solution)/shard_map/ppermute | solution.py:55
  58.0 1.1 %collective-permute-start.13 = (f32[286,2,2]{2,0,1:T(8,128)S(1)}, f32[286,2,2]{2,0,1:T(8,128)S(1)}, u32[]{:S(2)}, u32[]{:S(2)}) collective-permute-start(f32[286,2,2]{2,0,1:T(8,128)S(1)} %get-tuple-element.31), channel_id=1, source_target_pairs={{0,2},{2,4},{4,6},{6,0},{1,3},{3,5},{5,7},{7,1},{8,10},{10,12},{12... | collective-permute-start | bytes 13736 | tf_op jit(solution)/shard_map/ppermute | solution.py:55
  59.0 4.5 %collective-permute-done.14 = f32[286,2,2]{2,0,1:T(8,128)S(1)} collective-permute-done((f32[286,2,2]{2,0,1:T(8,128)S(1)}, f32[286,2,2]{2,0,1:T(8,128)S(1)}, u32[]{:S(2)}, u32[]{:S(2)}) %collective-permute-start.14) | collective-permute-done | bytes 4608 | tf_op jit(solution)/shard_map/ppermute | solution.py:55
  63.5 0.7 slice_bitcast_fusion.2
  64.2 3.9 %collective-permute-done.13 = f32[286,2,2]{2,0,1:T(8,128)S(1)} collective-permute-done((f32[286,2,2]{2,0,1:T(8,128)S(1)}, f32[286,2,2]{2,0,1:T(8,128)S(1)}, u32[]{:S(2)}, u32[]{:S(2)}) %collective-permute-start.13) | collective-permute-done | bytes 4608 | tf_op jit(solution)/shard_map/ppermute | solution.py:55
  68.1 0.7 slice_bitcast_fusion.4
  68.9 0.7 slice_bitcast_fusion.6
  69.6 0.7 slice_bitcast_fusion.10
  70.4 1.6 %concatenate.54 = f32[286,776]{1,0:T(8,128)S(1)} concatenate(f32[286,128]{1,0:T(8,128)} %get-tuple-element.39, f32[286,128]{1,0:T(8,128)} %get-tuple-element.38, f32[286,128]{1,0:T(8,128)} %get-tuple-element.37, f32[286,128]{1,0:T(8,128)} %get-tuple-element.36, f32[286,128]{1,0:T(8,128)} %get-tuple-element.35, f32[286,128]{1,0:T(8,128)} %get-tuple-element.34, ...), dimensions={1} | concatenate | bytes 1775488 | tf_op jit(solution)/shard_map/concatenate | solution.py:95
  72.0 2.7 %fusion.67 = f32[512,776]{0,1:T(8,128)S(1)} fusion(f32[286,512]{1,0:T(8,128)S(1)} %convolution_reduce_fusion, f32[286,776]{1,0:T(8,128)S(1)} %concatenate.54), kind=kOutput, calls=%fused_computation.128 | convolution fusion | flops 1363574784 | bytes 3062720 | tf_op jit(solution)/shard_map/dot_general | solution.py:93
  74.9 0.7 copy-done.3
  75.7 0.4 fusion.37
  76.0 0.7 fusion
  76.7 0.2 reshape.26
  76.9 0.9 %copy.65 = f32[286,2,128]{2,1,0:T(2,128)} copy(f32[286,2,128]{2,0,1:T(8,128)S(1)} %fusion.12) | data formatting | bytes 585728 | tf_op jit(solution)/shard_map/add | solution.py:117
  (52 shorter events, 1.9 us)
Async XLA Ops:
  1.0 10.4 %copy-start.4 = (s32[512,10]{0,1:T(8,128)S(1)}, s32[512,10]{0,1:T(8,128)}, u32[]{:S(2)}) copy-start(s32[512,10]{0,1:T(8,128)} %param.10) | copy-start | bytes 61444
  1.0 10.5 %copy-start.6 = (f32[4]{0:T(128)S(1)}, f32[4]{0:T(128)}, u32[]{:S(2)}) copy-start(f32[4]{0:T(128)} %constant.91.clone) | copy-start | bytes 52
  1.0 11.9 %copy-start.5 = (f32[4,4,1]{1,0,2:T(4,128)S(1)}, f32[4,4,1]{1,0,2:T(4,128)}, u32[]{:S(2)}) copy-start(f32[4,4,1]{1,0,2:T(4,128)} %constant.105) | copy-start | bytes 196
  2.0 11.1 %copy-start.7 = (s32[286,10]{0,1:T(8,128)S(1)}, s32[286,10]{0,1:T(8,128)}, u32[]{:S(2)}) copy-start(s32[286,10]{0,1:T(8,128)} %param.11) | copy-start | bytes 34324
  2.1 41.1 %collective-permute-start.6 = (f32[286,2,128]{2,0,1:T(8,128)S(1)}, f32[286,2,128]{2,0,1:T(8,128)}, u32[]{:S(2)}, u32[]{:S(2)}) collective-permute-start(f32[286,2,128]{2,0,1:T(8,128)S(1)} %copy.54), channel_id=1, source_target_pairs={{1,0},{8,1},{9,8},{16,9},{17,16},{24,17},{25,24},{0,25},{3,2},{10,... | collective-permute-start | bytes 878600 | tf_op jit(solution)/shard_map/ppermute | solution.py:55
  6.6 38.3 %collective-permute-start.5 = (f32[286,2,128]{2,0,1:T(8,128)S(1)}, f32[286,2,128]{2,0,1:T(8,128)}, u32[]{:S(2)}, u32[]{:S(2)}) collective-permute-start(f32[286,2,128]{2,0,1:T(8,128)S(1)} %copy.54), channel_id=1, source_target_pairs={{0,1},{1,8},{8,9},{9,16},{16,17},{17,24},{24,25},{25,0},{2,3},{3,1... | collective-permute-start | bytes 878600 | tf_op jit(solution)/shard_map/ppermute | solution.py:55
  6.7 31.2 %collective-permute-start.2 = (f32[1,128,1,2,128]{4,3,0,1,2:T(2,128)S(1)}, f32[1,128,1,2,128]{4,3,0,1,2:T(2,128)S(1)}, u32[]{:S(2)}, u32[]{:S(2)}) collective-permute-start(f32[1,128,1,2,128]{4,3,0,1,2:T(2,128)S(1)} %get-tuple-element.25), channel_id=1, source_target_pairs={{0,24},{8,0},{16,8},{24,16},{1,25},{9,1},{17,9},{25,17},{2,26},{10... | collective-permute-start | bytes 393224 | tf_op jit(solution)/shard_map/ppermute | solution.py:72
  7.9 22.1 %collective-permute-start = (f32[1,128,1,2,128]{4,3,0,1,2:T(2,128)S(1)}, f32[1,128,1,2,128]{4,3,0,1,2:T(2,128)S(1)}, u32[]{:S(2)}, u32[]{:S(2)}) collective-permute-start(f32[1,128,1,2,128]{4,3,0,1,2:T(2,128)S(1)} %get-tuple-element.26), channel_id=1, source_target_pairs={{0,8},{8,16},{16,24},{24,0},{1,9},{9,17},{17,25},{25,1},{2,10},{10... | collective-permute-start | bytes 393224 | tf_op jit(solution)/shard_map/ppermute | solution.py:72
  9.0 9.3 %collective-permute-start.8 = (f32[286,2,2]{2,0,1:T(8,128)S(1)}, f32[286,2,2]{2,0,1:T(8,128)S(1)}, u32[]{:S(2)}, u32[]{:S(2)}) collective-permute-start(f32[286,2,2]{2,0,1:T(8,128)S(1)} %get-tuple-element.42), channel_id=1, source_target_pairs={{2,0},{4,2},{6,4},{0,6},{3,1},{5,3},{7,5},{1,7},{10,8},{12,10},{14... | collective-permute-start | bytes 13736 | tf_op jit(solution)/shard_map/ppermute | solution.py:55
  18.3 11.0 %collective-permute-start.7 = (f32[286,2,2]{2,0,1:T(8,128)S(1)}, f32[286,2,2]{2,0,1:T(8,128)S(1)}, u32[]{:S(2)}, u32[]{:S(2)}) collective-permute-start(f32[286,2,2]{2,0,1:T(8,128)S(1)} %get-tuple-element.43), channel_id=1, source_target_pairs={{0,2},{2,4},{4,6},{6,0},{1,3},{3,5},{5,7},{7,1},{8,10},{10,12},{12... | collective-permute-start | bytes 13736 | tf_op jit(solution)/shard_map/ppermute | solution.py:55
  29.2 8.6 %collective-permute-start.1 = (f32[1,128,1,2,128]{4,3,0,1,2:T(2,128)S(1)}, f32[1,128,1,2,128]{4,3,0,1,2:T(2,128)S(1)}, u32[]{:S(2)}, u32[]{:S(2)}) collective-permute-start(f32[1,128,1,2,128]{4,3,0,1,2:T(2,128)S(1)} %get-tuple-element.27), channel_id=1, source_target_pairs={{0,16},{8,24},{16,0},{24,8},{1,17},{9,25},{17,1},{25,9},{2,18},{10... | collective-permute-start | bytes 393224 | tf_op jit(solution)/shard_map/ppermute | solution.py:72
  38.5 4.6 %collective-permute-start.3 = (f32[512,2,1]{0,2,1:T(1,128)S(1)}, f32[512,2,1]{0,2,1:T(1,128)S(1)}, u32[]{:S(2)}, u32[]{:S(2)}) collective-permute-start(f32[512,2,1]{0,2,1:T(1,128)S(1)} %get-tuple-element.23), channel_id=1, source_target_pairs={{0,2},{2,4},{4,6},{6,0},{1,3},{3,5},{5,7},{7,1},{8,10},{10,12},{12... | collective-permute-start | bytes 12296 | tf_op jit(solution)/shard_map/ppermute | solution.py:55
  39.5 3.7 %collective-permute-start.4 = (f32[512,2,1]{0,2,1:T(1,128)S(1)}, f32[512,2,1]{0,2,1:T(1,128)S(1)}, u32[]{:S(2)}, u32[]{:S(2)}) collective-permute-start(f32[512,2,1]{0,2,1:T(1,128)S(1)} %get-tuple-element.24), channel_id=1, source_target_pairs={{2,0},{4,2},{6,4},{0,6},{3,1},{5,3},{7,5},{1,7},{10,8},{12,10},{14... | collective-permute-start | bytes 12296 | tf_op jit(solution)/shard_map/ppermute | solution.py:55
  41.6 9.5 %collective-permute-start.10 = (f32[512,128]{0,1:T(8,128)S(1)}, f32[512,128]{0,1:T(8,128)S(1)}, u32[]{:S(2)}, u32[]{:S(2)}) collective-permute-start(f32[512,128]{0,1:T(8,128)S(1)} %get-tuple-element.21), channel_id=1, source_target_pairs={{1,0},{8,1},{9,8},{16,9},{17,16},{24,17},{25,24},{0,25},{3,2},{10,... | collective-permute-start | bytes 786440 | tf_op jit(solution)/shard_map/ppermute | solution.py:55
  43.1 8.0 %collective-permute-start.9 = (f32[512,128]{0,1:T(8,128)S(1)}, f32[512,128]{0,1:T(8,128)S(1)}, u32[]{:S(2)}, u32[]{:S(2)}) collective-permute-start(f32[512,128]{0,1:T(8,128)S(1)} %get-tuple-element.22), channel_id=1, source_target_pairs={{0,1},{1,8},{8,9},{9,16},{16,17},{17,24},{24,25},{25,0},{2,3},{3,1... | collective-permute-start | bytes 786440 | tf_op jit(solution)/shard_map/ppermute | solution.py:55
  51.1 0.7 copy-start.2
  51.8 1.0 %copy-start = (f32[286,2,128]{2,1,0:T(2,128)S(1)}, f32[286,2,128]{2,1,0:T(2,128)}, u32[]{:S(2)}) copy-start(f32[286,2,128]{2,1,0:T(2,128)} %param.7) | copy-start | bytes 878596
  51.8 1.0 %copy-start.1 = (f32[286,2,128]{2,1,0:T(2,128)S(1)}, f32[286,2,128]{2,1,0:T(2,128)}, u32[]{:S(2)}) copy-start(f32[286,2,128]{2,1,0:T(2,128)} %param.8) | copy-start | bytes 878596
  53.1 10.4 %collective-permute-start.14 = (f32[286,2,2]{2,0,1:T(8,128)S(1)}, f32[286,2,2]{2,0,1:T(8,128)S(1)}, u32[]{:S(2)}, u32[]{:S(2)}) collective-permute-start(f32[286,2,2]{2,0,1:T(8,128)S(1)} %get-tuple-element.30), channel_id=1, source_target_pairs={{2,0},{4,2},{6,4},{0,6},{3,1},{5,3},{7,5},{1,7},{10,8},{12,10},{14... | collective-permute-start | bytes 13736 | tf_op jit(solution)/shard_map/ppermute | solution.py:55
  56.8 12.1 %collective-permute-start.12 = (f32[286,2,128]{2,0,1:T(8,128)S(1)}, f32[286,2,128]{2,0,1:T(8,128)S(1)}, u32[]{:S(2)}, u32[]{:S(2)}) collective-permute-start(f32[286,2,128]{2,0,1:T(8,128)S(1)} %fusion.15), channel_id=1, source_target_pairs={{1,0},{8,1},{9,8},{16,9},{17,16},{24,17},{25,24},{0,25},{3,2},{10,... | collective-permute-start | bytes 878600 | tf_op jit(solution)/shard_map/ppermute | solution.py:55
  58.0 11.6 %collective-permute-start.11 = (f32[286,2,128]{2,0,1:T(8,128)S(1)}, f32[286,2,128]{2,0,1:T(8,128)S(1)}, u32[]{:S(2)}, u32[]{:S(2)}) collective-permute-start(f32[286,2,128]{2,0,1:T(8,128)S(1)} %fusion.15), channel_id=1, source_target_pairs={{0,1},{1,8},{8,9},{9,16},{16,17},{17,24},{24,25},{25,0},{2,3},{3,1... | collective-permute-start | bytes 878600 | tf_op jit(solution)/shard_map/ppermute | solution.py:55
  58.0 10.1 %collective-permute-start.13 = (f32[286,2,2]{2,0,1:T(8,128)S(1)}, f32[286,2,2]{2,0,1:T(8,128)S(1)}, u32[]{:S(2)}, u32[]{:S(2)}) collective-permute-start(f32[286,2,2]{2,0,1:T(8,128)S(1)} %get-tuple-element.31), channel_id=1, source_target_pairs={{0,2},{2,4},{4,6},{6,0},{1,3},{3,5},{5,7},{7,1},{8,10},{10,12},{12... | collective-permute-start | bytes 13736 | tf_op jit(solution)/shard_map/ppermute | solution.py:55
  74.7 1.0 %copy-start.3 = (f32[512,128]{0,1:T(8,128)S(1)}, f32[512,128]{0,1:T(8,128)}, u32[]{:S(2)}) copy-start(f32[512,128]{0,1:T(8,128)} %copy-done.2) | copy-start | bytes 786436
